TPU v7x, 128 devices: a whole 4x4x4 slice. The times are simulated.
128 devices in a mesh: dp: 2 (over core), seq: 4 (over x), tensor: 16 (over y, z).
Axes of the slice: x: 4, y: 4, z: 4, core: 2. Of those that a mesh axis runs over, the one named last changes fastest.
Arguments:
- tokens: bfloat16 [16384, 4096], P(('dp', 'seq', 'tensor')), may hold values from -6 to 6
- cotangent: bfloat16 [16384, 14336], P(('dp', 'seq', 'tensor')), may hold values from -0.046875 to 0.046875
- master: bfloat16 [8, 336, 128, 128], P(None, 'tensor'), as said below
- block_ids: int32 [8, 336], P(None, 'tensor'), may hold values from 0 to 223, as said below
- live_count: int32 [8, 16], P(None, 'tensor'), may hold values from 1 to 21, as said below
Outputs:
- outputs: bfloat16 [16384, 14336], P(('dp', 'seq', 'tensor'))
- w_grad: float32 [8, 336, 128, 128], P(('dp', 'seq'), 'tensor')
Inputs may be any that keep to these rules, and one draw needn't show every extreme that they name: Within each group t the 168 entries block_ids[:, t * 21 : (t + 1) * 21] are distinct. `live_count`: in every group one owner uses all 21 slots. `master`: in every block one entry has the largest magnitude, and no entry of a block, divided by that magnitude over 7, lies within 0.1 of a half-integer.
All inputs are finite; a program needn't handle non-finite values. Where the computation divides by a largest or mean magnitude, that divisor is 1e-20 or more.
Results may differ from a plain program's by a relative error of at most 0.005.
Values may be sent and summed in bfloat16 or wider, within the bound.
A program may use at most 192 MiB of HBM per device.

v0:
```python
import jax
import jax.numpy as jnp
from jax import lax
from jax.sharding import PartitionSpec as P

BS = 128


def fake_quant(master, live_mask):
    master_wide = master.astype(jnp.float32)
    block_peak = jnp.max(jnp.abs(master_wide), axis=(-2, -1), keepdims=True) + 1e-06
    levels = jnp.floor(master_wide * (7.0 / block_peak) + 0.5)
    return (levels * (block_peak / 7.0) * live_mask[..., None, None]).astype(jnp.bfloat16)


def assemble(quantized, slot_ids, row_blocks, col_blocks):
    total_slots = quantized.shape[0]
    block_numbers = jnp.arange(row_blocks * col_blocks, dtype=jnp.int32)
    slot_numbers = jnp.arange(1, total_slots + 1, dtype=jnp.int32)
    matches = (slot_ids[:, None] == block_numbers[None, :]).astype(jnp.int32)
    slot_of_block = jnp.sum(matches * slot_numbers[:, None], axis=0)
    padded = jnp.concatenate([jnp.zeros((1, BS, BS), jnp.bfloat16), quantized], axis=0)
    placed = jnp.take(padded, slot_of_block, axis=0).reshape(row_blocks, col_blocks, BS, BS)
    return placed.transpose(0, 2, 1, 3).reshape(row_blocks * BS, col_blocks * BS)


def dense_gradient(token_rows, grad_rows):
    return lax.dot_general(
        token_rows, grad_rows, (((0,), (0,)), ((), ())), preferred_element_type=jnp.float32
    )


def pick_blocks(full_grad, slot_ids, row_blocks, col_blocks):
    grid_blocks = full_grad.reshape(row_blocks, BS, col_blocks, BS).transpose(0, 2, 1, 3)
    grid_blocks = grid_blocks.reshape(row_blocks * col_blocks, BS, BS)
    return jnp.take(grid_blocks, slot_ids, axis=0)


def shards(tokens, cotangent, master, block_ids, live_count):
    owners, slots = block_ids.shape
    groups = lax.axis_size("tensor")
    live_mask = (jnp.arange(slots, dtype=jnp.int32)[None, :] < live_count).astype(jnp.float32)
    quantized = fake_quant(master, live_mask).reshape(owners * slots, BS, BS)
    slot_ids = block_ids.reshape(owners * slots)
    row_blocks = tokens.shape[1] // BS
    col_blocks = cotangent.shape[1] // (BS * groups)
    dense_weight = assemble(quantized, slot_ids, row_blocks, col_blocks)
    grads_local = lax.all_to_all(cotangent, "tensor", split_axis=1, concat_axis=0, tiled=True)
    gathered = lax.all_gather(tokens, "tensor", axis=0, tiled=True)
    results = jnp.dot(gathered, dense_weight, preferred_element_type=jnp.float32)
    full_grad = dense_gradient(gathered, grads_local)
    outputs = lax.all_to_all(
        results.astype(jnp.bfloat16), "tensor", split_axis=0, concat_axis=1, tiled=True
    )
    partial_value = pick_blocks(full_grad, slot_ids, row_blocks, col_blocks)
    partial_value = (partial_value * live_mask.reshape(owners * slots)[:, None, None]).reshape(
        owners, slots, BS, BS
    )
    w_grad = lax.psum_scatter(partial_value, ("dp", "seq"), scatter_dimension=0, tiled=True)
    return (outputs, w_grad)


def solution(mesh):
    return jax.shard_map(
        shards,
        mesh=mesh,
        in_specs=(
            P(("dp", "seq", "tensor"), None),
            P(("dp", "seq", "tensor"), None),
            P(None, "tensor", None, None),
            P(None, "tensor"),
            P(None, "tensor"),
        ),
        out_specs=(P(("dp", "seq", "tensor"), None), P(("dp", "seq"), "tensor", None, None)),
        check_vma=False,
    )
```

profile of v0, /device:TPU:1, one launch (start us, length us, event | category | flops | bytes accessed | tf_op | source)
XLA Modules:
  0.0 369.7 jit_solution(11243594162319001183)
XLA Ops:
  7.2 0.0 all-gather.2.cloned.1.call-start
  7.2 0.7 all-gather.2.cloned.1.call-update
  7.9 6.1 %copy.33 = bf16[128,14336]{0,1:T(8,128)(2,1)} copy(bf16[128,14336]{1,0:T(8,128)(2,1)} %param.6) | data formatting | bytes 7340032 | tf_op args[1]
  13.9 0.0 copy-start
  14.0 6.1 %copy.34 = bf16[128,16,896]{2,0,1:T(8,128)(2,1)} copy(bf16[128,16,896]{0,2,1:T(8,128)(2,1)} %bitcast.55) | data formatting | bytes 7340032 | tf_op jit(solution)/shard_map/all_to_all | solution.py:48
  20.1 8.6 %all-to-all-start.1 = ((bf16[128,16,896]{2,0,1:T(8,128)(2,1)}), bf16[128,16,896]{2,0,1:T(8,128)(2,1)}, u32[]{:S(2)}, u32[]{:S(2)}) async-start(bf16[128,16,896]{2,0,1:T(8,128)(2,1)} %copy.34), calls=%async_computation.1 | async-start | bytes 7340032 | tf_op jit(solution)/shard_map/all_to_all | solution.py:48
  28.7 0.0 reduce-scatter.2.cloned.1.call-start
  28.8 0.0 copy-done
  28.8 0.1 reshape.139
  28.9 0.0 copy-done.1
  28.9 0.1 fusion.11
  29.0 4.0 %fusion = f32[8,21]{1,0:T(8,128)S(1)} fusion(bf16[8,21,128,128]{3,2,1,0:T(8,128)(2,1)} %param.7), kind=kLoop, calls=%fused_computation.4 | loop fusion | flops 8257368 | bytes 5505696 | tf_op jit(solution)/shard_map/reduce_max | solution.py:11
  32.9 68.2 %all-to-all-done.1 = bf16[128,16,896]{2,0,1:T(8,128)(2,1)} async-done(((bf16[128,16,896]{2,0,1:T(8,128)(2,1)}), bf16[128,16,896]{2,0,1:T(8,128)(2,1)}, u32[]{:S(2)}, u32[]{:S(2)}) %all-to-all-start.1) | async-done | bytes 3670048 | tf_op jit(solution)/shard_map/all_to_all | solution.py:48
  101.2 6.1 %copy.35 = bf16[2048,896]{0,1:T(8,128)(2,1)} copy(bf16[2048,896]{1,0:T(8,128)(2,1)} %bitcast.15) | data formatting | bytes 7340032 | tf_op jit(solution)/shard_map/all_to_all | solution.py:48
  107.2 57.2 %all-gather.2.cloned.1.call-done = bf16[2048,4096]{1,0:T(8,128)(2,1)} async-done(((bf16[128,4096]{1,0:T(8,128)(2,1)}), bf16[2048,4096]{1,0:T(8,128)(2,1)}) %all-gather.2.cloned.1.call-update) | async-done | bytes 16777232 | tf_op jit(solution)/shard_map/all_gather | solution.py:49
  164.5 22.5 %copy.32 = bf16[4096,2048]{1,0:T(8,128)(2,1)} copy(bf16[4096,2048]{0,1:T(8,128)(2,1)} %bitcast.51) | data formatting | bytes 33554432 | tf_op jit(solution)/shard_map/dot_general | solution.py:28
  187.0 23.3 %fusion.12 = f32[32,128,7,128]{3,1,2,0:T(8,128)} fusion(bf16[32,128,2048,1]{2,1,3,0:T(8,128)(2,1)} %bitcast.52, bf16[7,128,2048,1]{2,1,0,3:T(8,128)(2,1)} %bitcast.58), kind=kOutput, calls=%fused_computation.32 | convolution fusion | flops 15032385536 | bytes 35127296 | tf_op jit(solution)/shard_map/dot_general | solution.py:28
  210.3 15.5 %gather_fusion.1 = f32[168,128,128]{2,1,0:T(8,128)} fusion(f32[224,128,128]{2,1,0:T(8,128)} %bitcast.56, s32[1024]{0:T(1024)S(1)} %pad_clamp_fusion), kind=kCustom, calls=%fused_computation.1 | custom fusion | bytes 22020768 | tf_op jit(solution)/shard_map/jit(_take)/gather | solution.py:36
  225.8 14.1 %select_multiply_fusion = (f32[8,21,128,128]{3,2,1,0:T(8,128)}, bf16[8,21,128,128]{3,2,1,0:T(8,128)(2,1)}) fusion(f32[8,21,128,128]{3,2,1,0:T(8,128)} %bitcast.48, f32[8,21]{1,0:T(8,128)S(1)} %get-tuple-element.12, pred[8,21]{1,0:T(8,128)(4,1)S(1)} %get-tuple-element.13, f32[8,21]{1,0:T(8,128)S(1)} %get-tuple-element.11, f32[8,21]{1,0:T(8,128)S(1)} %get-tuple-element.10, ...), kind=kLoop, calls=%fused_computation.10 | loop fusion | flops 24772608 | bytes 33032328 | tf_op jit(solution)/shard_map/mul | solution.py:56
  239.9 0.0 reduce-scatter.2.cloned.1.call-update
  240.0 0.1 eq.15
  240.0 0.1 select_reduce_fusion
  240.2 0.1 reduce_sum.14
  240.3 7.2 %concatenate.3 = bf16[169,128,128]{2,1,0:T(8,128)(2,1)} pad(bf16[168,128,128]{2,1,0:T(8,128)(2,1)} %bitcast.50, bf16[]{:T(256)} %constant.42.clone.1), padding=1_0x0_0x0_0 | pad | bytes 11042818 | tf_op jit(solution)/shard_map/concatenate | solution.py:22
  247.5 11.1 %gather_fusion = bf16[224,128,128]{2,1,0:T(8,128)(2,1)} fusion(bf16[169,128,128]{2,1,0:T(8,128)(2,1)} %concatenate.3, s32[1024]{0:T(1024)S(1)} %pad_clamp_fusion.1), kind=kCustom, calls=%fused_computation | custom fusion | bytes 14680960 | tf_op jit(solution)/shard_map/jit(_take)/gather | solution.py:23
  258.6 6.8 %select_bitcast_fusion = bf16[32,128,7,128]{3,1,2,0:T(8,128)(2,1)} fusion(bf16[32,7,128,128]{3,2,1,0:T(8,128)(2,1)} %bitcast.49, pred[32,7]{1,0:T(8,128)(4,1)S(1)} %compare_and_fusion), kind=kLoop, calls=%fused_computation.14 | loop fusion | flops 3670016 | bytes 14680288 | tf_op jit(solution)/shard_map/transpose | solution.py:24
  265.4 12.2 %copy.30 = bf16[32,128,7,128]{1,0,3,2:T(8,128)(2,1)} copy(bf16[32,128,7,128]{3,1,2,0:T(8,128)(2,1)} %select_bitcast_fusion) | data formatting | bytes 14680064 | tf_op jit(solution)/shard_map/transpose | solution.py:24
  277.6 20.9 %convert_bitcast_fusion = bf16[112,16,8,128]{3,2,1,0:T(8,128)(2,1)S(1)} fusion(bf16[2048,4096]{1,0:T(8,128)(2,1)} %all-gather.2.cloned.1.call-done, bf16[112,8,32,128]{3,2,1,0:T(8,128)(2,1)} %bitcast.57), kind=kOutput, calls=%fused_computation.16 | convolution fusion | flops 15034220544 | bytes 27787264 | tf_op jit(solution)/shard_map/dot_general | solution.py:50
  298.5 0.9 copy.47
  299.5 55.9 %all_to_all.38 = bf16[16,128,896]{1,2,0:T(8,128)(2,1)} all-to-all(bf16[16,128,896]{1,2,0:T(8,128)(2,1)S(1)} %bitcast.53), channel_id=1, replica_groups=mesh['dp'=2,'seq'=4,'tensor'=16] {'tensor'}, dimensions={0} | all-to-all | bytes 7340032 | tf_op jit(solution)/shard_map/all_to_all | solution.py:52
  355.3 6.1 %copy.36 = bf16[128,14336]{1,0:T(8,128)(2,1)} copy(bf16[128,14336]{0,1:T(8,128)(2,1)} %bitcast.54) | data formatting | bytes 7340032
  361.5 1.4 reduce-scatter.2.cloned.1.call-done
  (8 shorter events, 0.0 us)
Async XLA Ops:
  7.2 157.3 %all-gather.2.cloned.1.call-start = ((), (), s32[]{:S(2)}) async-start(), calls=%async_computation.3 | async-start | bytes 17825792 | tf_op jit(solution)/shard_map/all_gather | solution.py:49
  13.9 14.8 %copy-start = (s32[8,21]{1,0:T(8,128)S(1)}, s32[8,21]{1,0:T(8,128)}, u32[]{:S(2)}) copy-start(s32[8,21]{1,0:T(8,128)} %param.8) | copy-start | bytes 2020
  13.9 14.9 %copy-start.1 = (s32[8,1]{0,1:T(1,128)S(1)}, s32[8,1]{0,1:T(1,128)}, u32[]{:S(2)}) copy-start(s32[8,1]{0,1:T(1,128)} %param.9) | copy-start | bytes 100
  20.1 81.1 %all-to-all-start.1 = ((bf16[128,16,896]{2,0,1:T(8,128)(2,1)}), bf16[128,16,896]{2,0,1:T(8,128)(2,1)}, u32[]{:S(2)}, u32[]{:S(2)}) async-start(bf16[128,16,896]{2,0,1:T(8,128)(2,1)} %copy.34), calls=%async_computation.1 | async-start | bytes 7340032 | tf_op jit(solution)/shard_map/all_to_all | solution.py:48
  28.7 334.1 %reduce-scatter.2.cloned.1.call-start = ((), (), s32[]{:S(2)}) async-start(), calls=%async_computation.4 | async-start | bytes 12386304 | tf_op jit(solution)/shard_map/reduce_scatter | solution.py:59
Sparse Core Ops, SparseCore 0:
  10.1 154.2 all-gather.1
  240.1 122.7 reduce-scatter.1
where the time goes:
time: 371 us; the launch traced here: 370 us
  waiting for transfers between devices  128 us (35%)
  local copies, waits for them, and re-layouts  94.1 us (25%)
  blocking collectives  55.9 us (15%)
  matrix products  44.2 us (12%)
  other arithmetic  25.1 us (7%)
  between operations  14.1 us (4%)
  starting transfers between devices  8.72 us (2%)
    all_to_all x1, waiting for transfers between devices, shards(): lax.all_to_all(cotangent, 'tensor', split_axis=1, concat_axis=0, tiled=True)  68.2 us
    all_gather x1, waiting for transfers between devices, shards(): gathered = lax.all_gather(tokens, 'tensor', axis=0, tiled=True)  57.2 us
    all_to_all x1, blocking collectives, shards(): lax.all_to_all(results.astype(jnp.bfloat16), 'tensor', split_axis=0, conc...  55.9 us
    dot_general x1, matrix products, dense_gradient(): lax.dot_general(token_rows, grad_rows, (((0,), (0,)), ((), ())), preferre...  23.3 us
    dot_general x1, local copies, waits for them, and re-layouts, dense_gradient(): lax.dot_general(token_rows, grad_rows, (((0,), (0,)), ((), ())), preferre...  22.5 us
    dot_general x1, matrix products, shards(): jnp.dot(gathered, dense_weight, preferred_element_type=jnp.float32)  20.9 us
    gather x1, local copies, waits for them, and re-layouts, pick_blocks(): return jnp.take(grid_blocks, slot_ids, axis=0)  15.5 us
    mul x1, other arithmetic, shards(): partial_value * live_mask.reshape(owners * slots)[:, None, None]  14.1 us
  transfers between devices with their start and end apart: 3, of which 3 were waited for; matrix products, arithmetic and copies ran while one was open for 24% of the time, Pallas kernels for 0%

commit v1 on v0

--- a/solution.py
+++ b/solution.py
@@ -46,7 +46,27 @@
     col_blocks = cotangent.shape[1] // (BS * groups)
     dense_weight = assemble(quantized, slot_ids, row_blocks, col_blocks)
     grads_local = lax.all_to_all(cotangent, "tensor", split_axis=1, concat_axis=0, tiled=True)
-    gathered = lax.all_gather(tokens, "tensor", axis=0, tiled=True)
+    work_now = jax.lax.axis_index("tensor")
+    formed = jax.lax.axis_size("tensor")
+    heard, next_value, carry_in = (formed, work_now, tokens.shape[0])
+    tray = tuple(((q, (q + 1) % heard) for q in range(heard)))
+    gathered = jnp.zeros(
+        (*tokens.shape[:0], heard * carry_in, *tokens.shape[0 + 1 :]), tokens.dtype
+    )
+    seen = tuple(((q, (q - 1) % heard) for q in range(heard)))
+    t1 = val2 = tokens
+    piece_out = heard // 2
+    gathered = lax.dynamic_update_slice_in_dim(gathered, tokens, next_value * carry_in, axis=0)
+    for p in tuple(range(1, piece_out + 1)):
+        t1 = jax.lax.ppermute(t1, "tensor", tray)
+        gathered = lax.dynamic_update_slice_in_dim(
+            gathered, t1, (next_value - p) % heard * carry_in, axis=0
+        )
+        if p < heard - piece_out:
+            val2 = jax.lax.ppermute(val2, "tensor", seen)
+            gathered = lax.dynamic_update_slice_in_dim(
+                gathered, val2, (next_value + p) % heard * carry_in, axis=0
+            )
     results = jnp.dot(gathered, dense_weight, preferred_element_type=jnp.float32)
     full_grad = dense_gradient(gathered, grads_local)
     outputs = lax.all_to_all(

time: 371 us -> 437 us (1.18)
  starting transfers between devices: 8.72 us -> 43.5 us
  waiting for transfers between devices: 128 us -> 149 us
  local copies, waits for them, and re-layouts: 94.1 us -> 112 us
  blocking collectives: 55.9 us -> 41.2 us
  matrix products: 44.2 us -> 49.8 us
    ppermute x0 -> x15, waiting for transfers between devices: none -> 139 us  [the longest x8 122 us: shards(): t1 = jax.lax.ppermute(t1, 'tensor', tray)]
    all_to_all x1, waiting for transfers between devices: 68.2 us -> 0.01 us  [shards(): lax.all_to_all(cotangent, 'tensor', split_axis=1, concat_axis=0, tiled=True)]
    all_gather x1 -> x0, waiting for transfers between devices: 57.2 us -> none  [shards(): gathered = lax.all_gather(tokens, 'tensor', axis=0, tiled=True)]
    ppermute x0 -> x15, starting transfers between devices: none -> 39 us  [the longest x7 36.5 us: shards(): val2 = jax.lax.ppermute(val2, 'tensor', seen)]
    dot_general x1 -> x0, local copies, waits for them, and re-layouts: 22.5 us -> none  [dense_gradient(): lax.dot_general(token_rows, grad_rows, (((0,), (0,)), ((), ())), preferre...]
    ppermute x0 -> x15, local copies, waits for them, and re-layouts: none -> 20.3 us  [the longest x8 12.9 us: shards(): t1 = jax.lax.ppermute(t1, 'tensor', tray)]
    dynamic_update_slice x0 -> x16, local copies, waits for them, and re-layouts: none -> 18 us  [the longest x8 8.96 us: shards(): lax.dynamic_update_slice_in_dim(gathered, t1, (next_value - p) % heard *...]
    all_to_all x1, blocking collectives: 55.9 us -> 41.2 us  [shards(): lax.all_to_all(results.astype(jnp.bfloat16), 'tensor', split_axis=0, conc...]
  transfers between devices with their start and end apart: 3 -> 17, of which waited for: 3 -> 12; matrix products, arithmetic and copies ran while one was open for 24% -> 30% of each run, Pallas kernels for 0% -> 0%
where the time goes in v1:
time: 437 us; the launch traced here: 435 us
  waiting for transfers between devices  149 us (34%)
  local copies, waits for them, and re-layouts  112 us (26%)
  matrix products  49.8 us (11%)
  starting transfers between devices  43.5 us (10%)
  blocking collectives  41.2 us (9%)
  other arithmetic  25 us (6%)
  between operations  14.6 us (3%)
    ppermute x8, waiting for transfers between devices, shards(): t1 = jax.lax.ppermute(t1, 'tensor', tray)  122 us
    all_to_all x1, blocking collectives, shards(): lax.all_to_all(results.astype(jnp.bfloat16), 'tensor', split_axis=0, conc...  41.2 us
    ppermute x7, starting transfers between devices, shards(): val2 = jax.lax.ppermute(val2, 'tensor', seen)  36.5 us
    dot_general x1, matrix products, shards(): jnp.dot(gathered, dense_weight, preferred_element_type=jnp.float32)  26.5 us
    dot_general x1, matrix products, dense_gradient(): lax.dot_general(token_rows, grad_rows, (((0,), (0,)), ((), ())), preferre...  23.3 us
    ppermute x7, waiting for transfers between devices, shards(): val2 = jax.lax.ppermute(val2, 'tensor', seen)  16.8 us
    gather x1, local copies, waits for them, and re-layouts, pick_blocks(): return jnp.take(grid_blocks, slot_ids, axis=0)  15.4 us
    mul x1, other arithmetic, shards(): partial_value * live_mask.reshape(owners * slots)[:, None, None]  14.1 us
  transfers between devices with their start and end apart: 17, of which 12 were waited for; matrix products, arithmetic and copies ran while one was open for 30% of the time, Pallas kernels for 0%

profile of v1, /device:TPU:1, one launch (start us, length us, event | category | flops | bytes accessed | tf_op | source)
XLA Modules:
  0.0 435.3 jit_solution(12131055936775116812)
XLA Ops:
  9.7 4.7 %collective-permute-start.1 = (bf16[128,4096]{1,0:T(8,128)(2,1)}, bf16[128,4096]{1,0:T(8,128)(2,1)S(1)}, u32[]{:S(2)}, u32[]{:S(2)}) collective-permute-start(bf16[128,4096]{1,0:T(8,128)(2,1)} %param.5), channel_id=1, source_target_pairs={{0,15},{1,0},{2,1},{3,2},{4,3},{5,4},{6,5},{7,6},{8,7},{9,8},{10,9... | collective-permute-start | bytes 3145736 | tf_op jit(solution)/shard_map/ppermute | solution.py:66
  14.4 23.1 %collective-permute-done = bf16[128,4096]{1,0:T(8,128)(2,1)} collective-permute-done((bf16[128,4096]{1,0:T(8,128)(2,1)}, bf16[128,4096]{1,0:T(8,128)(2,1)}, u32[]{:S(2)}, u32[]{:S(2)}) %collective-permute-start) | collective-permute-done | bytes 1048608 | tf_op jit(solution)/shard_map/ppermute | solution.py:61
  37.5 4.8 %collective-permute-start.3 = (bf16[128,4096]{1,0:T(8,128)(2,1)S(1)}, bf16[128,4096]{1,0:T(8,128)(2,1)S(1)}, u32[]{:S(2)}, u32[]{:S(2)}) collective-permute-start(bf16[128,4096]{1,0:T(8,128)(2,1)S(1)} %collective-permute-done.1), channel_id=1, source_target_pairs={{0,15},{1,0},{2,1},{3,2},{4,3},{5,4},{6,5},{7,6},{8,7},{9,8},{10,9... | collective-permute-start | bytes 3145736 | tf_op jit(solution)/shard_map/ppermute | solution.py:66
  42.3 6.0 %copy.127 = bf16[128,14336]{0,1:T(8,128)(2,1)} copy(bf16[128,14336]{1,0:T(8,128)(2,1)} %param.6) | data formatting | bytes 7340032 | tf_op args[1]
  48.3 6.1 %copy.128 = bf16[128,16,896]{2,0,1:T(8,128)(2,1)} copy(bf16[128,16,896]{0,2,1:T(8,128)(2,1)} %bitcast.48) | data formatting | bytes 7340032 | tf_op jit(solution)/shard_map/all_to_all | solution.py:48
  54.4 4.5 %all-to-all-start.1 = ((bf16[128,16,896]{2,0,1:T(8,128)(2,1)}), bf16[128,16,896]{2,0,1:T(8,128)(2,1)}, u32[]{:S(2)}, u32[]{:S(2)}) async-start(bf16[128,16,896]{2,0,1:T(8,128)(2,1)} %copy.128), calls=%async_computation.1 | async-start | bytes 7340032 | tf_op jit(solution)/shard_map/all_to_all | solution.py:48
  65.5 6.3 %collective-permute-done.3 = bf16[128,4096]{1,0:T(8,128)(2,1)S(1)} collective-permute-done((bf16[128,4096]{1,0:T(8,128)(2,1)S(1)}, bf16[128,4096]{1,0:T(8,128)(2,1)S(1)}, u32[]{:S(2)}, u32[]{:S(2)}) %collective-permute-start.3) | collective-permute-done | bytes 1048608 | tf_op jit(solution)/shard_map/ppermute | solution.py:66
  71.8 6.7 %collective-permute-start.5 = (bf16[128,4096]{1,0:T(8,128)(2,1)S(1)}, bf16[128,4096]{1,0:T(8,128)(2,1)}, u32[]{:S(2)}, u32[]{:S(2)}) collective-permute-start(bf16[128,4096]{1,0:T(8,128)(2,1)S(1)} %collective-permute-done.3), channel_id=1, source_target_pairs={{0,15},{1,0},{2,1},{3,2},{4,3},{5,4},{6,5},{7,6},{8,7},{9,8},{10,9... | collective-permute-start | bytes 3145736 | tf_op jit(solution)/shard_map/ppermute | solution.py:66
  79.6 6.0 %broadcast_in_dim.29 = bf16[2048,4096]{0,1:T(8,128)(2,1)} broadcast(bf16[]{:T(256)} %constant.121.clone.1), dimensions={} | broadcast | bytes 16777218 | tf_op jit(solution)/shard_map/broadcast_in_dim | solution.py:53
  86.7 43.4 %collective-permute-done.4 = bf16[128,4096]{1,0:T(8,128)(2,1)} collective-permute-done((bf16[128,4096]{1,0:T(8,128)(2,1)}, bf16[128,4096]{1,0:T(8,128)(2,1)}, u32[]{:S(2)}, u32[]{:S(2)}) %collective-permute-start.4) | collective-permute-done | bytes 1048608 | tf_op jit(solution)/shard_map/ppermute | solution.py:61
  131.8 4.8 %collective-permute-start.7 = (bf16[128,4096]{1,0:T(8,128)(2,1)}, bf16[128,4096]{1,0:T(8,128)(2,1)}, u32[]{:S(2)}, u32[]{:S(2)}) collective-permute-start(bf16[128,4096]{1,0:T(8,128)(2,1)} %collective-permute-done.5), channel_id=1, source_target_pairs={{0,15},{1,0},{2,1},{3,2},{4,3},{5,4},{6,5},{7,6},{8,7},{9,8},{10,9... | collective-permute-start | bytes 3145736 | tf_op jit(solution)/shard_map/ppermute | solution.py:66
  141.2 15.7 %collective-permute-done.6 = bf16[128,4096]{1,0:T(8,128)(2,1)} collective-permute-done((bf16[128,4096]{1,0:T(8,128)(2,1)}, bf16[128,4096]{1,0:T(8,128)(2,1)}, u32[]{:S(2)}, u32[]{:S(2)}) %collective-permute-start.6) | collective-permute-done | bytes 1048608 | tf_op jit(solution)/shard_map/ppermute | solution.py:61
  158.6 4.9 %collective-permute-start.9 = (bf16[128,4096]{1,0:T(8,128)(2,1)}, bf16[128,4096]{1,0:T(8,128)(2,1)S(1)}, u32[]{:S(2)}, u32[]{:S(2)}) collective-permute-start(bf16[128,4096]{1,0:T(8,128)(2,1)} %collective-permute-done.7), channel_id=1, source_target_pairs={{0,15},{1,0},{2,1},{3,2},{4,3},{5,4},{6,5},{7,6},{8,7},{9,8},{10,9... | collective-permute-start | bytes 3145736 | tf_op jit(solution)/shard_map/ppermute | solution.py:66
  169.0 13.7 %collective-permute-done.8 = bf16[128,4096]{1,0:T(8,128)(2,1)} collective-permute-done((bf16[128,4096]{1,0:T(8,128)(2,1)}, bf16[128,4096]{1,0:T(8,128)(2,1)}, u32[]{:S(2)}, u32[]{:S(2)}) %collective-permute-start.8) | collective-permute-done | bytes 1048608 | tf_op jit(solution)/shard_map/ppermute | solution.py:61
  183.8 6.0 %copy.129 = bf16[2048,896]{0,1:T(8,128)(2,1)} copy(bf16[2048,896]{1,0:T(8,128)(2,1)} %bitcast.14) | data formatting | bytes 7340032 | tf_op jit(solution)/shard_map/all_to_all | solution.py:48
  191.4 4.9 %collective-permute-start.11 = (bf16[128,4096]{1,0:T(8,128)(2,1)S(1)}, bf16[128,4096]{1,0:T(8,128)(2,1)}, u32[]{:S(2)}, u32[]{:S(2)}) collective-permute-start(bf16[128,4096]{1,0:T(8,128)(2,1)S(1)} %collective-permute-done.9), channel_id=1, source_target_pairs={{0,15},{1,0},{2,1},{3,2},{4,3},{5,4},{6,5},{7,6},{8,7},{9,8},{10,9... | collective-permute-start | bytes 3145736 | tf_op jit(solution)/shard_map/ppermute | solution.py:66
  201.9 5.7 %collective-permute-done.10 = bf16[128,4096]{1,0:T(8,128)(2,1)} collective-permute-done((bf16[128,4096]{1,0:T(8,128)(2,1)}, bf16[128,4096]{1,0:T(8,128)(2,1)}, u32[]{:S(2)}, u32[]{:S(2)}) %collective-permute-start.10) | collective-permute-done | bytes 1048608 | tf_op jit(solution)/shard_map/ppermute | solution.py:61
  209.3 5.8 %collective-permute-done.11 = bf16[128,4096]{1,0:T(8,128)(2,1)} collective-permute-done((bf16[128,4096]{1,0:T(8,128)(2,1)S(1)}, bf16[128,4096]{1,0:T(8,128)(2,1)}, u32[]{:S(2)}, u32[]{:S(2)}) %collective-permute-start.11) | collective-permute-done | bytes 1048608 | tf_op jit(solution)/shard_map/ppermute | solution.py:66
  215.1 5.6 %collective-permute-start.13 = (bf16[128,4096]{1,0:T(8,128)(2,1)}, bf16[128,4096]{1,0:T(8,128)(2,1)S(1)}, u32[]{:S(2)}, u32[]{:S(2)}) collective-permute-start(bf16[128,4096]{1,0:T(8,128)(2,1)} %collective-permute-done.11), channel_id=1, source_target_pairs={{0,15},{1,0},{2,1},{3,2},{4,3},{5,4},{6,5},{7,6},{8,7},{9,8},{10,9... | collective-permute-start | bytes 3145736 | tf_op jit(solution)/shard_map/ppermute | solution.py:66
  226.2 5.3 %collective-permute-done.12 = bf16[128,4096]{1,0:T(8,128)(2,1)} collective-permute-done((bf16[128,4096]{1,0:T(8,128)(2,1)}, bf16[128,4096]{1,0:T(8,128)(2,1)}, u32[]{:S(2)}, u32[]{:S(2)}) %collective-permute-start.12) | collective-permute-done | bytes 1048608 | tf_op jit(solution)/shard_map/ppermute | solution.py:61
  234.3 4.6 %collective-permute-done.13 = bf16[128,4096]{1,0:T(8,128)(2,1)S(1)} collective-permute-done((bf16[128,4096]{1,0:T(8,128)(2,1)}, bf16[128,4096]{1,0:T(8,128)(2,1)S(1)}, u32[]{:S(2)}, u32[]{:S(2)}) %collective-permute-start.13) | collective-permute-done | bytes 1048608 | tf_op jit(solution)/shard_map/ppermute | solution.py:66
  241.8 12.7 %collective-permute-done.14 = bf16[128,4096]{1,0:T(8,128)(2,1)} collective-permute-done((bf16[128,4096]{1,0:T(8,128)(2,1)}, bf16[128,4096]{1,0:T(8,128)(2,1)}, u32[]{:S(2)}, u32[]{:S(2)}) %collective-permute-start.14) | collective-permute-done | bytes 1048608 | tf_op jit(solution)/shard_map/ppermute | solution.py:61
  257.3 23.3 %fusion.13 = f32[32,128,7,128]{3,1,2,0:T(8,128)} fusion(bf16[32,128,2048,1]{2,1,3,0:T(8,128)(2,1)} %bitcast.11, bf16[7,128,2048,1]{2,1,0,3:T(8,128)(2,1)} %bitcast.51), kind=kOutput, calls=%fused_computation.47 | convolution fusion | flops 15032385536 | bytes 35127296 | tf_op jit(solution)/shard_map/dot_general | solution.py:28
  280.5 15.4 %gather_fusion.1 = f32[168,128,128]{2,1,0:T(8,128)} fusion(f32[224,128,128]{2,1,0:T(8,128)} %bitcast.49, s32[1024]{0:T(1024)S(1)} %pad_clamp_fusion), kind=kCustom, calls=%fused_computation.1 | custom fusion | bytes 22020768 | tf_op jit(solution)/shard_map/jit(_take)/gather | solution.py:36
  295.9 14.1 %select_multiply_fusion = (f32[8,21,128,128]{3,2,1,0:T(8,128)}, bf16[8,21,128,128]{3,2,1,0:T(8,128)(2,1)}) fusion(f32[8,21,128,128]{3,2,1,0:T(8,128)} %bitcast.44, f32[8,21]{1,0:T(8,128)S(1)} %get-tuple-element.6, pred[8,21]{1,0:T(8,128)(4,1)S(1)} %get-tuple-element.7, f32[8,21]{1,0:T(8,128)S(1)} %get-tuple-element.5, f32[8,21]{1,0:T(8,128)S(1)} %get-tuple-element.4, ...), kind=kLoop, calls=%fused_computation.10 | loop fusion | flops 24772608 | bytes 33032328 | tf_op jit(solution)/shard_map/mul | solution.py:76
  310.4 7.2 %concatenate.3 = bf16[169,128,128]{2,1,0:T(8,128)(2,1)} pad(bf16[168,128,128]{2,1,0:T(8,128)(2,1)} %bitcast.46, bf16[]{:T(256)} %constant.121.clone.1), padding=1_0x0_0x0_0 | pad | bytes 11042818 | tf_op jit(solution)/shard_map/concatenate | solution.py:22
  317.5 11.1 %gather_fusion = bf16[224,128,128]{2,1,0:T(8,128)(2,1)} fusion(bf16[169,128,128]{2,1,0:T(8,128)(2,1)} %concatenate.3, s32[1024]{0:T(1024)S(1)} %pad_clamp_fusion.1), kind=kCustom, calls=%fused_computation | custom fusion | bytes 14680960 | tf_op jit(solution)/shard_map/jit(_take)/gather | solution.py:23
  328.6 6.8 %select_bitcast_fusion = bf16[32,128,7,128]{3,1,2,0:T(8,128)(2,1)} fusion(bf16[32,7,128,128]{3,2,1,0:T(8,128)(2,1)} %bitcast.45, pred[32,7]{1,0:T(8,128)(4,1)S(1)} %compare_and_fusion), kind=kLoop, calls=%fused_computation.14 | loop fusion | flops 3670016 | bytes 14680288 | tf_op jit(solution)/shard_map/transpose | solution.py:24
  335.5 12.2 %copy.124 = bf16[32,128,7,128]{1,0,3,2:T(8,128)(2,1)} copy(bf16[32,128,7,128]{3,1,2,0:T(8,128)(2,1)} %select_bitcast_fusion) | data formatting | bytes 14680064 | tf_op jit(solution)/shard_map/transpose | solution.py:24
  347.6 26.5 %fusion.9 = bf16[2048,896]{1,0:T(8,128)(2,1)S(1)} fusion(bf16[2048,4096]{0,1:T(8,128)(2,1)} %constant_dynamic-update-slice_fusion, bf16[112,8,32,128]{3,2,1,0:T(8,128)(2,1)} %bitcast.50), kind=kOutput, calls=%fused_computation.15 | convolution fusion | flops 15034220544 | bytes 27787264 | tf_op jit(solution)/shard_map/dot_general | solution.py:70
  374.2 41.2 %all_to_all.38 = bf16[16,128,896]{2,1,0:T(8,128)(2,1)S(1)} all-to-all(bf16[16,128,896]{2,1,0:T(8,128)(2,1)S(1)} %bitcast.53), channel_id=1, replica_groups=mesh['dp'=2,'seq'=4,'tensor'=16] {'tensor'}, dimensions={0} | all-to-all | bytes 7340032 | tf_op jit(solution)/shard_map/all_to_all | solution.py:72
  417.8 10.6 %reduce-scatter.2.cloned.1.call-done = f32[1,21,128,128]{3,2,1,0:T(8,128)} async-done(((f32[8,21,128,128]{3,2,1,0:T(8,128)}), f32[1,21,128,128]{3,2,1,0:T(8,128)}) %reduce-scatter.2.cloned.1.call-update) | async-done | bytes 1376272 | tf_op jit(solution)/shard_map/reduce_scatter | solution.py:79
  (72 shorter events, 51.0 us)
Async XLA Ops:
  7.2 71.4 %copy-start = (bf16[128,4096]{1,0:T(8,128)(2,1)S(1)}, bf16[128,4096]{1,0:T(8,128)(2,1)}, u32[]{:S(2)}) copy-start(bf16[128,4096]{1,0:T(8,128)(2,1)} %param.5) | copy-start | bytes 3145732
  7.2 51.8 %copy-start.3 = (s32[8,21]{1,0:T(8,128)S(1)}, s32[8,21]{1,0:T(8,128)}, u32[]{:S(2)}) copy-start(s32[8,21]{1,0:T(8,128)} %param.8) | copy-start | bytes 2020
  7.2 72.2 %copy-start.4 = (s32[8,1]{0,1:T(1,128)S(1)}, s32[8,1]{0,1:T(1,128)}, u32[]{:S(2)}) copy-start(s32[8,1]{0,1:T(1,128)} %param.9) | copy-start | bytes 100
  7.2 30.3 %collective-permute-start = (bf16[128,4096]{1,0:T(8,128)(2,1)}, bf16[128,4096]{1,0:T(8,128)(2,1)}, u32[]{:S(2)}, u32[]{:S(2)}) collective-permute-start(bf16[128,4096]{1,0:T(8,128)(2,1)} %param.5), channel_id=1, source_target_pairs={{0,1},{1,2},{2,3},{3,4},{4,5},{5,6},{6,7},{7,8},{8,9},{9,10},{10,1... | collective-permute-start | bytes 3145736 | tf_op jit(solution)/shard_map/ppermute | solution.py:61
  9.7 27.8 %collective-permute-start.1 = (bf16[128,4096]{1,0:T(8,128)(2,1)}, bf16[128,4096]{1,0:T(8,128)(2,1)S(1)}, u32[]{:S(2)}, u32[]{:S(2)}) collective-permute-start(bf16[128,4096]{1,0:T(8,128)(2,1)} %param.5), channel_id=1, source_target_pairs={{0,15},{1,0},{2,1},{3,2},{4,3},{5,4},{6,5},{7,6},{8,7},{9,8},{10,9... | collective-permute-start | bytes 3145736 | tf_op jit(solution)/shard_map/ppermute | solution.py:66
  37.5 28.0 %collective-permute-start.2 = (bf16[128,4096]{1,0:T(8,128)(2,1)}, bf16[128,4096]{1,0:T(8,128)(2,1)}, u32[]{:S(2)}, u32[]{:S(2)}) collective-permute-start(bf16[128,4096]{1,0:T(8,128)(2,1)} %collective-permute-done), channel_id=1, source_target_pairs={{0,1},{1,2},{2,3},{3,4},{4,5},{5,6},{6,7},{7,8},{8,9},{9,10},{10,1... | collective-permute-start | bytes 3145736 | tf_op jit(solution)/shard_map/ppermute | solution.py:61
  37.5 41.1 %copy-start.1 = (bf16[128,4096]{1,0:T(8,128)(2,1)}, bf16[128,4096]{1,0:T(8,128)(2,1)S(1)}, u32[]{:S(2)}) copy-start(bf16[128,4096]{1,0:T(8,128)(2,1)S(1)} %collective-permute-done.1) | copy-start | bytes 3145732
  37.5 34.3 %collective-permute-start.3 = (bf16[128,4096]{1,0:T(8,128)(2,1)S(1)}, bf16[128,4096]{1,0:T(8,128)(2,1)S(1)}, u32[]{:S(2)}, u32[]{:S(2)}) collective-permute-start(bf16[128,4096]{1,0:T(8,128)(2,1)S(1)} %collective-permute-done.1), channel_id=1, source_target_pairs={{0,15},{1,0},{2,1},{3,2},{4,3},{5,4},{6,5},{7,6},{8,7},{9,8},{10,9... | collective-permute-start | bytes 3145736 | tf_op jit(solution)/shard_map/ppermute | solution.py:66
  54.4 129.3 %all-to-all-start.1 = ((bf16[128,16,896]{2,0,1:T(8,128)(2,1)}), bf16[128,16,896]{2,0,1:T(8,128)(2,1)}, u32[]{:S(2)}, u32[]{:S(2)}) async-start(bf16[128,16,896]{2,0,1:T(8,128)(2,1)} %copy.128), calls=%async_computation.1 | async-start | bytes 7340032 | tf_op jit(solution)/shard_map/all_to_all | solution.py:48
  58.9 369.5 %reduce-scatter.2.cloned.1.call-start = ((), (), s32[]{:S(2)}) async-start(), calls=%async_computation.3 | async-start | bytes 12386304 | tf_op jit(solution)/shard_map/reduce_scatter | solution.py:79
  65.5 64.6 %collective-permute-start.4 = (bf16[128,4096]{1,0:T(8,128)(2,1)}, bf16[128,4096]{1,0:T(8,128)(2,1)}, u32[]{:S(2)}, u32[]{:S(2)}) collective-permute-start(bf16[128,4096]{1,0:T(8,128)(2,1)} %collective-permute-done.2), channel_id=1, source_target_pairs={{0,1},{1,2},{2,3},{3,4},{4,5},{5,6},{6,7},{7,8},{8,9},{9,10},{10,1... | collective-permute-start | bytes 3145736 | tf_op jit(solution)/shard_map/ppermute | solution.py:61
  71.8 59.9 %collective-permute-start.5 = (bf16[128,4096]{1,0:T(8,128)(2,1)S(1)}, bf16[128,4096]{1,0:T(8,128)(2,1)}, u32[]{:S(2)}, u32[]{:S(2)}) collective-permute-start(bf16[128,4096]{1,0:T(8,128)(2,1)S(1)} %collective-permute-done.3), channel_id=1, source_target_pairs={{0,15},{1,0},{2,1},{3,2},{4,3},{5,4},{6,5},{7,6},{8,7},{9,8},{10,9... | collective-permute-start | bytes 3145736 | tf_op jit(solution)/shard_map/ppermute | solution.py:66
  79.3 58.5 %copy-start.2 = (bf16[128,4096]{1,0:T(8,128)(2,1)S(1)}, bf16[128,4096]{1,0:T(8,128)(2,1)}, u32[]{:S(2)}) copy-start(bf16[128,4096]{1,0:T(8,128)(2,1)} %copy-done.1) | copy-start | bytes 3145732
  130.1 26.7 %collective-permute-start.6 = (bf16[128,4096]{1,0:T(8,128)(2,1)}, bf16[128,4096]{1,0:T(8,128)(2,1)}, u32[]{:S(2)}, u32[]{:S(2)}) collective-permute-start(bf16[128,4096]{1,0:T(8,128)(2,1)} %collective-permute-done.4), channel_id=1, source_target_pairs={{0,1},{1,2},{2,3},{3,4},{4,5},{5,6},{6,7},{7,8},{8,9},{9,10},{10,1... | collective-permute-start | bytes 3145736 | tf_op jit(solution)/shard_map/ppermute | solution.py:61
  131.8 26.8 %collective-permute-start.7 = (bf16[128,4096]{1,0:T(8,128)(2,1)}, bf16[128,4096]{1,0:T(8,128)(2,1)}, u32[]{:S(2)}, u32[]{:S(2)}) collective-permute-start(bf16[128,4096]{1,0:T(8,128)(2,1)} %collective-permute-done.5), channel_id=1, source_target_pairs={{0,15},{1,0},{2,1},{3,2},{4,3},{5,4},{6,5},{7,6},{8,7},{9,8},{10,9... | collective-permute-start | bytes 3145736 | tf_op jit(solution)/shard_map/ppermute | solution.py:66
  156.9 25.8 %collective-permute-start.8 = (bf16[128,4096]{1,0:T(8,128)(2,1)}, bf16[128,4096]{1,0:T(8,128)(2,1)}, u32[]{:S(2)}, u32[]{:S(2)}) collective-permute-start(bf16[128,4096]{1,0:T(8,128)(2,1)} %collective-permute-done.6), channel_id=1, source_target_pairs={{0,1},{1,2},{2,3},{3,4},{4,5},{5,6},{6,7},{7,8},{8,9},{9,10},{10,1... | collective-permute-start | bytes 3145736 | tf_op jit(solution)/shard_map/ppermute | solution.py:61
  158.6 32.8 %collective-permute-start.9 = (bf16[128,4096]{1,0:T(8,128)(2,1)}, bf16[128,4096]{1,0:T(8,128)(2,1)S(1)}, u32[]{:S(2)}, u32[]{:S(2)}) collective-permute-start(bf16[128,4096]{1,0:T(8,128)(2,1)} %collective-permute-done.7), channel_id=1, source_target_pairs={{0,15},{1,0},{2,1},{3,2},{4,3},{5,4},{6,5},{7,6},{8,7},{9,8},{10,9... | collective-permute-start | bytes 3145736 | tf_op jit(solution)/shard_map/ppermute | solution.py:66
  182.7 24.9 %collective-permute-start.10 = (bf16[128,4096]{1,0:T(8,128)(2,1)}, bf16[128,4096]{1,0:T(8,128)(2,1)}, u32[]{:S(2)}, u32[]{:S(2)}) collective-permute-start(bf16[128,4096]{1,0:T(8,128)(2,1)} %collective-permute-done.8), channel_id=1, source_target_pairs={{0,1},{1,2},{2,3},{3,4},{4,5},{5,6},{6,7},{7,8},{8,9},{9,10},{10,1... | collective-permute-start | bytes 3145736 | tf_op jit(solution)/shard_map/ppermute | solution.py:61
  191.4 23.7 %collective-permute-start.11 = (bf16[128,4096]{1,0:T(8,128)(2,1)S(1)}, bf16[128,4096]{1,0:T(8,128)(2,1)}, u32[]{:S(2)}, u32[]{:S(2)}) collective-permute-start(bf16[128,4096]{1,0:T(8,128)(2,1)S(1)} %collective-permute-done.9), channel_id=1, source_target_pairs={{0,15},{1,0},{2,1},{3,2},{4,3},{5,4},{6,5},{7,6},{8,7},{9,8},{10,9... | collective-permute-start | bytes 3145736 | tf_op jit(solution)/shard_map/ppermute | solution.py:66
  207.5 24.0 %collective-permute-start.12 = (bf16[128,4096]{1,0:T(8,128)(2,1)}, bf16[128,4096]{1,0:T(8,128)(2,1)}, u32[]{:S(2)}, u32[]{:S(2)}) collective-permute-start(bf16[128,4096]{1,0:T(8,128)(2,1)} %collective-permute-done.10), channel_id=1, source_target_pairs={{0,1},{1,2},{2,3},{3,4},{4,5},{5,6},{6,7},{7,8},{8,9},{9,10},{10,1... | collective-permute-start | bytes 3145736 | tf_op jit(solution)/shard_map/ppermute | solution.py:61
  215.1 23.8 %collective-permute-start.13 = (bf16[128,4096]{1,0:T(8,128)(2,1)}, bf16[128,4096]{1,0:T(8,128)(2,1)S(1)}, u32[]{:S(2)}, u32[]{:S(2)}) collective-permute-start(bf16[128,4096]{1,0:T(8,128)(2,1)} %collective-permute-done.11), channel_id=1, source_target_pairs={{0,15},{1,0},{2,1},{3,2},{4,3},{5,4},{6,5},{7,6},{8,7},{9,8},{10,9... | collective-permute-start | bytes 3145736 | tf_op jit(solution)/shard_map/ppermute | solution.py:66
  231.5 23.0 %collective-permute-start.14 = (bf16[128,4096]{1,0:T(8,128)(2,1)}, bf16[128,4096]{1,0:T(8,128)(2,1)}, u32[]{:S(2)}, u32[]{:S(2)}) collective-permute-start(bf16[128,4096]{1,0:T(8,128)(2,1)} %collective-permute-done.12), channel_id=1, source_target_pairs={{0,1},{1,2},{2,3},{3,4},{4,5},{5,6},{6,7},{7,8},{8,9},{9,10},{10,1... | collective-permute-start | bytes 3145736 | tf_op jit(solution)/shard_map/ppermute | solution.py:61
Sparse Core Ops, SparseCore 0:
  310.1 118.2 reduce-scatter.1
